TPU v7x, 32 devices: a whole 2x2x4 slice. The times are simulated.
32 devices in a mesh: seq: 2 (over x), hist: 8 (over z, y), chan: 2 (over core).
Axes of the slice: x: 2, y: 2, z: 4, core: 2. Of those that a mesh axis runs over, the one named last changes fastest.
Arguments:
- history: bfloat16 [4096, 4096], P(('seq', 'hist'), 'chan'), parts along dimension 0, may hold values from -6 to 6
- filter_taps: bfloat16 [2048, 4096], P('hist', 'chan'), may hold values from -0.125 to 0.125
- gate_values: bfloat16 [512, 4096], P(('seq', 'hist'), 'chan'), parts along dimension 0, may hold values from -6 to 6
- out_weight: bfloat16 [4096, 4096], P('chan', 'hist'), may hold values from -0.09375 to 0.09375
Outputs:
- output: bfloat16 [512, 4096], P(('seq', 'hist', 'chan')), parts along dimension 0
There are 2 independent parts, one for each index of `seq`. A program takes and returns all parts, laid end to end along the dimension named above; an argument that names none is the same for every part. Nothing has to cross between parts.
All inputs are finite; a program needn't handle non-finite values.
Results may differ from a plain program's by a relative error of at most 0.013.
Values may be sent and summed in bfloat16 or wider, within the bound.
A program may use at most 64 MiB of HBM per device.

v0:
```python
import math
import jax
import jax.numpy as jnp
from jax import lax
from jax.sharding import PartitionSpec as P


def shifted(value, axis, steps):
    count = lax.axis_size(axis)
    initial, last = (max(0, -steps), min(count, count - steps))
    return lax.ppermute(value, axis, [(source, source + steps) for source in range(initial, last)])


def split_product(table_high, table_low, values):
    first = jnp.dot(table_high, values, preferred_element_type=jnp.float32)
    return first + jnp.dot(table_low, values, preferred_element_type=jnp.float32)


def inverse_part(real_part, imag_part, block_tokens, period, row_count):
    scale = 2.0 * math.pi / period
    lags = block_tokens - 1 - lax.broadcasted_iota(jnp.int32, (row_count, period), 0)
    orders = lax.broadcasted_iota(jnp.int32, (row_count, period), 1)
    phases = (lags * orders % period).astype(jnp.float32) * scale
    cosines = jnp.dot(
        jnp.cos(phases),
        real_part,
        precision=lax.Precision.HIGHEST,
        preferred_element_type=jnp.float32,
    )
    sines = jnp.dot(
        jnp.sin(phases),
        imag_part,
        precision=lax.Precision.HIGHEST,
        preferred_element_type=jnp.float32,
    )
    return (cosines - sines) / period


def local(history, filter_taps, gate_values, out_weight):
    local_rows, channels = history.shape
    owned_rows = gate_values.shape[0]
    count_hist = lax.axis_size("hist")
    count_chan = lax.axis_size("chan")
    block_tokens = owned_rows * count_hist
    period = local_rows + block_tokens
    next_taps = shifted(filter_taps, "hist", -1)
    extended = jnp.concatenate([filter_taps, next_taps], 0)
    scale = 2.0 * math.pi / period
    modes = lax.broadcasted_iota(jnp.int32, (period, period), 0)
    places = lax.broadcasted_iota(jnp.int32, (period, period), 1)
    angles = (modes * places % period).astype(jnp.float32) * scale
    table = jnp.concatenate([jnp.cos(angles), jnp.sin(angles)], 0)
    table_high = table.astype(jnp.bfloat16)
    table_low = (table - table_high.astype(jnp.float32)).astype(jnp.bfloat16)
    spec_taps = split_product(table_high, table_low, extended)
    spec_input = split_product(table_high[:, :local_rows], table_low[:, :local_rows], history)
    taps_cos, taps_sin = (spec_taps[:period], spec_taps[period:])
    input_cos, input_sin = (spec_input[:period], spec_input[period:])
    real_part = taps_cos * input_cos + taps_sin * input_sin
    imag_part = taps_cos * input_sin - taps_sin * input_cos
    conv = lax.psum_scatter(
        inverse_part(
            real_part, imag_part, block_tokens, period, owned_rows * lax.axis_size("hist")
        ),
        "hist",
        scatter_dimension=0,
        tiled=True,
    )
    gated = (conv * gate_values.astype(jnp.float32)).astype(jnp.bfloat16)
    partial_value = jnp.dot(
        lax.all_gather(gated, "hist", axis=0, tiled=True),
        out_weight,
        preferred_element_type=jnp.float32,
    )
    columns = partial_value.shape[1]
    half_rows = owned_rows // count_chan
    ordered = partial_value.reshape(count_hist, count_chan, half_rows, columns).transpose(
        1, 0, 2, 3
    )
    ordered = ordered.reshape(count_chan * count_hist * half_rows, columns)
    summed = lax.psum_scatter(ordered.astype(jnp.bfloat16), "chan", scatter_dimension=0, tiled=True)
    output = lax.all_to_all(summed, "hist", split_axis=0, concat_axis=1, tiled=True)
    return output


def solution(mesh):
    return jax.shard_map(
        local,
        mesh=mesh,
        in_specs=(
            P(("seq", "hist"), "chan"),
            P("hist", "chan"),
            P(("seq", "hist"), "chan"),
            P("chan", "hist"),
        ),
        out_specs=P(("seq", "hist", "chan"), None),
        check_vma=False,
    )
```

profile of v0, /device:TPU:0, one launch (start us, length us, event | category | flops | bytes accessed | tf_op | source)
XLA Modules:
  0.0 194.6 jit_solution(3666349346221288854)
XLA Ops:
  6.5 0.0 copy-start
  6.5 0.0 reduce-scatter.3.cloned.1.call-start
  6.5 1.5 collective-permute-start
  8.1 4.1 %fusion.36 = (f32[512,512]{1,0:T(8,128)S(1)}, f32[512,512]{1,0:T(8,128)S(1)}) fusion(), kind=kLoop, calls=%fused_computation.43 | loop fusion | flops 3670016 | bytes 2097152 | tf_op jit(solution)/shard_map/sin | solution.py:52
  12.2 0.3 subtract_convert_fusion
  12.5 0.1 fusion.22
  12.6 0.0 copy-done.1
  12.6 0.0 copy-start.2
  12.6 1.3 fusion.33
  13.9 0.0 copy-done.2
  13.9 0.1 constant_dynamic-update-slice_fusion.1
  14.0 1.4 convolution_add_fusion
  15.5 19.6 %collective-permute-done = bf16[256,2048]{1,0:T(8,128)(2,1)S(1)} collective-permute-done((bf16[256,2048]{1,0:T(8,128)(2,1)}, bf16[256,2048]{1,0:T(8,128)(2,1)S(1)}, u32[]{:S(2)}, u32[]{:S(2)}) %collective-permute-start) | collective-permute-done | bytes 1048608 | tf_op jit(solution)/shard_map/ppermute | solution.py:11
  35.1 0.1 constant_dynamic-update-slice_fusion
  35.2 2.4 %fusion.53 = f32[1024,2048]{1,0:T(8,128)S(1)} fusion(bf16[1024,512]{1,0:T(8,128)(2,1)S(1)} %subtract_convert_fusion, bf16[512,2048]{1,0:T(8,128)(2,1)S(1)} %constant_dynamic-update-slice_fusion), kind=kOutput, calls=%fused_computation.61 | convolution fusion | flops 2147483648 | bytes 11534336 | tf_op jit(solution)/shard_map/dot_general | solution.py:16
  37.5 2.4 %convolution_add_fusion.1 = f32[1024,2048]{1,0:T(8,128)S(1)} fusion(f32[1024,2048]{1,0:T(8,128)S(1)} %fusion.53, bf16[512,2048]{1,0:T(8,128)(2,1)S(1)} %constant_dynamic-update-slice_fusion, f32[512,512]{1,0:T(8,128)S(1)} %get-tuple-element.5, f32[512,512]{1,0:T(8,128)S(1)} %get-tuple-element.6), kind=kOutput, calls=%fused_computation.17 | convolution fusion | flops 2151677952 | bytes 20971520 | tf_op jit(solution)/shard_map/dot_general | solution.py:15
  39.9 6.2 %fusion = f32[256,2048]{1,0:T(8,128)S(1)} fusion(f32[1024,2048]{1,0:T(8,128)S(1)} %convolution_add_fusion, f32[1024,2048]{1,0:T(8,128)S(1)} %convolution_add_fusion.1, s32[256]{0:T(256)S(1)} %iota_subtract_fusion), kind=kOutput, calls=%fused_computation.1 | convolution fusion | flops 3226206208 | bytes 18875392 | tf_op jit(solution)/shard_map/dot_general | solution.py:30
  46.2 0.0 copy-start.3
  46.2 7.4 %fusion.19 = f32[256,2048]{1,0:T(8,128)} fusion(f32[256,2048]{1,0:T(8,128)S(1)} %fusion, f32[1024,2048]{1,0:T(8,128)S(1)} %convolution_add_fusion, f32[1024,2048]{1,0:T(8,128)S(1)} %convolution_add_fusion.1, s32[256]{0:T(256)S(1)} %iota_subtract_fusion), kind=kOutput, calls=%fused_computation.19 | convolution fusion | flops 3227254784 | bytes 20972544 | tf_op jit(solution)/shard_map/dot_general | solution.py:24
  53.6 0.0 reduce-scatter.3.cloned.1.call-update
  53.6 0.0 all-gather.2.cloned.1.call-start
  53.7 69.8 %reduce-scatter.3.cloned.1.call-done = f32[32,2048]{1,0:T(8,128)} async-done(((f32[256,2048]{1,0:T(8,128)}), f32[32,2048]{1,0:T(8,128)}) %reduce-scatter.3.cloned.1.call-update) | async-done | bytes 262160 | tf_op jit(solution)/shard_map/reduce_scatter | solution.py:61
  123.4 1.6 multiply_convert_fusion
  125.1 0.0 all-gather.2.cloned.1.call-update
  125.1 0.0 reduce-scatter.5.cloned.1.call-start
  125.1 39.8 %all-gather.2.cloned.1.call-done = bf16[256,2048]{1,0:T(8,128)(2,1)} async-done(((bf16[32,2048]{1,0:T(8,128)(2,1)}), bf16[256,2048]{1,0:T(8,128)(2,1)}) %all-gather.2.cloned.1.call-update) | async-done | bytes 1048592 | tf_op jit(solution)/shard_map/all_gather | solution.py:71
  164.9 1.9 convolution_convert_fusion
  166.8 0.7 copy.6
  167.6 0.0 reduce-scatter.5.cloned.1.call-update
  167.6 6.6 %reduce-scatter.5.cloned.1.call-done = bf16[128,512]{1,0:T(8,128)(2,1)} async-done(((bf16[256,512]{1,0:T(8,128)(2,1)}), bf16[128,512]{1,0:T(8,128)(2,1)}) %reduce-scatter.5.cloned.1.call-update) | async-done | bytes 131088 | tf_op jit(solution)/shard_map/reduce_scatter | solution.py:81
  174.2 13.2 %all_to_all.19 = bf16[8,16,512]{2,1,0:T(8,128)(2,1)S(1)} all-to-all(bf16[8,16,512]{2,1,0:T(8,128)(2,1)} %bitcast.18), channel_id=1, replica_groups=mesh['seq'=2,'hist'=8,'chan'=2] {'hist'}, dimensions={0} | all-to-all | bytes 262144 | tf_op jit(solution)/shard_map/all_to_all | solution.py:82
  187.4 0.7 copy.8
  (4 shorter events, 0.0 us)
Async XLA Ops:
  6.5 158.4 %copy-start = (bf16[2048,512]{1,0:T(8,128)(2,1)S(1)}, bf16[2048,512]{1,0:T(8,128)(2,1)}, u32[]{:S(2)}) copy-start(bf16[2048,512]{1,0:T(8,128)(2,1)} %param.7) | copy-start | bytes 6291460
  6.5 6.1 %copy-start.1 = (bf16[256,2048]{1,0:T(8,128)(2,1)S(1)}, bf16[256,2048]{1,0:T(8,128)(2,1)}, u32[]{:S(2)}) copy-start(bf16[256,2048]{1,0:T(8,128)(2,1)} %param.4) | copy-start | bytes 3145732
  6.5 116.9 %reduce-scatter.3.cloned.1.call-start = ((), (), s32[]{:S(2)}) async-start(), calls=%async_computation.3 | async-start | bytes 2359296 | tf_op jit(solution)/shard_map/reduce_scatter | solution.py:61
  6.5 28.5 %collective-permute-start = (bf16[256,2048]{1,0:T(8,128)(2,1)}, bf16[256,2048]{1,0:T(8,128)(2,1)S(1)}, u32[]{:S(2)}, u32[]{:S(2)}) collective-permute-start(bf16[256,2048]{1,0:T(8,128)(2,1)} %param.5), channel_id=1, source_target_pairs={{2,0},{4,2},{6,4},{8,6},{10,8},{12,10},{14,12},{3,1},{5,3},{7,5},{... | collective-permute-start | bytes 3145736 | tf_op jit(solution)/shard_map/ppermute | solution.py:11
  12.6 1.3 copy-start.2
  46.2 77.3 %copy-start.3 = (bf16[32,2048]{1,0:T(8,128)(2,1)S(1)}, bf16[32,2048]{1,0:T(8,128)(2,1)}, u32[]{:S(2)}) copy-start(bf16[32,2048]{1,0:T(8,128)(2,1)} %param.6) | copy-start | bytes 393220
  53.6 111.3 %all-gather.2.cloned.1.call-start = ((), (), s32[]{:S(2)}) async-start(), calls=%async_computation.4 | async-start | bytes 1179648 | tf_op jit(solution)/shard_map/all_gather | solution.py:71
  125.1 49.1 %reduce-scatter.5.cloned.1.call-start = ((), (), s32[]{:S(2)}) async-start(), calls=%async_computation.5 | async-start | bytes 393216 | tf_op jit(solution)/shard_map/reduce_scatter | solution.py:81
Sparse Core Ops, SparseCore 0:
  53.7 69.6 reduce-scatter.2
  125.6 39.2 all-gather.1
  167.7 6.4 reduce-scatter.4
where the time goes:
time: 195 us
  waiting for transfers between devices  136 us (70%)
  matrix products  23 us (12%)
  blocking collectives  13.2 us (7%)
  between operations  13.2 us (7%)
  other arithmetic  6.15 us (3%)
    reduce_scatter x1, waiting for transfers between devices, local(): lax.psum_scatter(inverse_part(real_part, imag_part, block_tokens, period,...  69.8 us
    all_gather x1, waiting for transfers between devices, local(): lax.all_gather(gated, 'hist', axis=0, tiled=True)  39.8 us
    ppermute x1, waiting for transfers between devices, shifted(): lax.ppermute(value, axis, [(source, source + steps) for source in range(i...  19.6 us
    all_to_all x1, blocking collectives, local(): lax.all_to_all(summed, 'hist', split_axis=0, concat_axis=1, tiled=True)  13.2 us
    dot_general x1, matrix products, inverse_part(): jnp.dot(jnp.cos(phases), real_part, precision=lax.Precision.HIGHEST, pref...  7.43 us
    reduce_scatter x1, waiting for transfers between devices, local(): lax.psum_scatter(ordered.astype(jnp.bfloat16), 'chan', scatter_dimension=...  6.61 us
    dot_general x1, matrix products, inverse_part(): jnp.dot(jnp.sin(phases), imag_part, precision=lax.Precision.HIGHEST, pref...  6.21 us
    sin x1, other arithmetic, local(): table = jnp.concatenate([jnp.cos(angles), jnp.sin(angles)], 0)  4.09 us
  transfers between devices with their start and end apart: 4, of which 4 were waited for; matrix products, arithmetic and copies ran while one was open for 4% of the time, Pallas kernels for 0%

commit v1 on v0

--- a/solution.py
+++ b/solution.py
@@ -68,7 +68,9 @@
     )
     gated = (conv * gate_values.astype(jnp.float32)).astype(jnp.bfloat16)
     partial_value = jnp.dot(
-        lax.all_gather(gated, "hist", axis=0, tiled=True),
+        jnp.concatenate(
+            lax.all_to_all(jnp.stack([gated] * lax.axis_size("hist")), "hist", 0, 0), axis=0
+        ),
         out_weight,
         preferred_element_type=jnp.float32,
     )

time: 195 us -> 182 us (0.933)
  waiting for transfers between devices: 136 us -> 96.8 us
  blocking collectives: 13.2 us -> 40.6 us
    all_gather x1 -> x0, waiting for transfers between devices: 39.8 us -> none  [local(): lax.all_gather(gated, 'hist', axis=0, tiled=True)]
    all_to_all x0 -> x1, blocking collectives: none -> 27.4 us  [local(): lax.all_to_all(jnp.stack([gated] * lax.axis_size('hist')), 'hist', 0, 0)]
  transfers between devices with their start and end apart: 4 -> 3, of which waited for: 4 -> 3; matrix products, arithmetic and copies ran while one was open for 4% -> 4% of each run, Pallas kernels for 0% -> 0%
where the time goes in v1:
time: 182 us; the launch traced here: 181 us
  waiting for transfers between devices  96.8 us (53%)
  blocking collectives  40.6 us (22%)
  matrix products  21.7 us (12%)
  between operations  13.5 us (7%)
  other arithmetic  5.49 us (3%)
    reduce_scatter x1, waiting for transfers between devices, local(): lax.psum_scatter(inverse_part(real_part, imag_part, block_tokens, period,...  70.1 us
    all_to_all x1, blocking collectives, local(): lax.all_to_all(jnp.stack([gated] * lax.axis_size('hist')), 'hist', 0, 0)  27.4 us
    ppermute x1, waiting for transfers between devices, shifted(): lax.ppermute(value, axis, [(source, source + steps) for source in range(i...  19.7 us
    all_to_all x1, blocking collectives, local(): lax.all_to_all(summed, 'hist', split_axis=0, concat_axis=1, tiled=True)  13.2 us
    dot_general x1, matrix products, inverse_part(): jnp.dot(jnp.cos(phases), real_part, precision=lax.Precision.HIGHEST, pref...  7.46 us
    reduce_scatter x1, waiting for transfers between devices, local(): lax.psum_scatter(ordered.astype(jnp.bfloat16), 'chan', scatter_dimension=...  6.89 us
    dot_general x1, matrix products, inverse_part(): jnp.dot(jnp.sin(phases), imag_part, precision=lax.Precision.HIGHEST, pref...  6.25 us
    sin x1, other arithmetic, local(): table = jnp.concatenate([jnp.cos(angles), jnp.sin(angles)], 0)  4.09 us
  transfers between devices with their start and end apart: 3, of which 3 were waited for; matrix products, arithmetic and copies ran while one was open for 4% of the time, Pallas kernels for 0%

profile of v1, /device:TPU:0, one launch (start us, length us, event | category | flops | bytes accessed | tf_op | source)
XLA Modules:
  0.0 181.4 jit_solution(2131423143314403701)
XLA Ops:
  6.5 0.0 copy-start
  6.5 0.0 reduce-scatter.3.cloned.1.call-start
  6.5 1.5 collective-permute-start
  8.1 4.1 %fusion.44 = (f32[512,512]{1,0:T(8,128)S(1)}, f32[512,512]{1,0:T(8,128)S(1)}) fusion(), kind=kLoop, calls=%fused_computation.46 | loop fusion | flops 3670016 | bytes 2097152 | tf_op jit(solution)/shard_map/sin | solution.py:52
  12.2 0.3 subtract_convert_fusion
  12.5 0.1 fusion.24
  12.6 0.0 copy-done.1
  12.6 0.0 copy-start.2
  12.6 1.3 fusion.41
  13.9 0.0 copy-done.2
  13.9 0.1 constant_dynamic-update-slice_fusion.1
  14.0 1.3 convolution_add_fusion
  15.3 19.7 %collective-permute-done = bf16[256,2048]{1,0:T(8,128)(2,1)S(1)} collective-permute-done((bf16[256,2048]{1,0:T(8,128)(2,1)}, bf16[256,2048]{1,0:T(8,128)(2,1)S(1)}, u32[]{:S(2)}, u32[]{:S(2)}) %collective-permute-start) | collective-permute-done | bytes 1048608 | tf_op jit(solution)/shard_map/ppermute | solution.py:11
  35.1 0.1 constant_dynamic-update-slice_fusion
  35.1 2.3 %fusion.61 = f32[1024,2048]{1,0:T(8,128)S(1)} fusion(bf16[1024,512]{1,0:T(8,128)(2,1)S(1)} %subtract_convert_fusion, bf16[512,2048]{1,0:T(8,128)(2,1)S(1)} %constant_dynamic-update-slice_fusion), kind=kOutput, calls=%fused_computation.64 | convolution fusion | flops 2147483648 | bytes 11534336 | tf_op jit(solution)/shard_map/dot_general | solution.py:16
  37.5 2.4 %convolution_add_fusion.1 = f32[1024,2048]{1,0:T(8,128)S(1)} fusion(f32[1024,2048]{1,0:T(8,128)S(1)} %fusion.61, bf16[512,2048]{1,0:T(8,128)(2,1)S(1)} %constant_dynamic-update-slice_fusion, f32[512,512]{1,0:T(8,128)S(1)} %get-tuple-element.5, f32[512,512]{1,0:T(8,128)S(1)} %get-tuple-element.6), kind=kOutput, calls=%fused_computation.17 | convolution fusion | flops 2151677952 | bytes 20971520 | tf_op jit(solution)/shard_map/dot_general | solution.py:15
  39.9 6.2 %fusion = f32[256,2048]{1,0:T(8,128)S(1)} fusion(f32[1024,2048]{1,0:T(8,128)S(1)} %convolution_add_fusion, f32[1024,2048]{1,0:T(8,128)S(1)} %convolution_add_fusion.1, s32[256]{0:T(256)S(1)} %iota_subtract_fusion), kind=kOutput, calls=%fused_computation.1 | convolution fusion | flops 3226206208 | bytes 18875392 | tf_op jit(solution)/shard_map/dot_general | solution.py:30
  46.1 0.0 copy-start.3
  46.2 7.5 %fusion.19 = f32[256,2048]{1,0:T(8,128)} fusion(f32[256,2048]{1,0:T(8,128)S(1)} %fusion, f32[1024,2048]{1,0:T(8,128)S(1)} %convolution_add_fusion, f32[1024,2048]{1,0:T(8,128)S(1)} %convolution_add_fusion.1, s32[256]{0:T(256)S(1)} %iota_subtract_fusion), kind=kOutput, calls=%fused_computation.19 | convolution fusion | flops 3227254784 | bytes 20972544 | tf_op jit(solution)/shard_map/dot_general | solution.py:24
  53.6 0.0 reduce-scatter.3.cloned.1.call-update
  53.6 0.0 reduce-scatter.5.cloned.1.call-start
  53.7 70.1 %reduce-scatter.3.cloned.1.call-done = f32[32,2048]{1,0:T(8,128)} async-done(((f32[256,2048]{1,0:T(8,128)}), f32[32,2048]{1,0:T(8,128)}) %reduce-scatter.3.cloned.1.call-update) | async-done | bytes 262160 | tf_op jit(solution)/shard_map/reduce_scatter | solution.py:61
  123.8 0.0 copy-done.3
  123.8 1.0 multiply_convert_fusion
  124.8 0.1 stack.2
  124.9 27.4 %all_to_all.24 = bf16[8,32,2048]{2,1,0:T(8,128)(2,1)S(1)} all-to-all(bf16[8,32,2048]{2,1,0:T(8,128)(2,1)S(1)} %stack.2), channel_id=1, replica_groups=mesh['seq'=2,'hist'=8,'chan'=2] {'hist'}, dimensions={0} | all-to-all | bytes 2097152 | tf_op jit(solution)/shard_map/all_to_all | solution.py:72
  152.3 0.7 fusion.28
  153.0 0.7 copy.6
  153.8 0.0 reduce-scatter.5.cloned.1.call-update
  153.8 6.9 %reduce-scatter.5.cloned.1.call-done = bf16[128,512]{1,0:T(8,128)(2,1)} async-done(((bf16[256,512]{1,0:T(8,128)(2,1)}), bf16[128,512]{1,0:T(8,128)(2,1)}) %reduce-scatter.5.cloned.1.call-update) | async-done | bytes 131088 | tf_op jit(solution)/shard_map/reduce_scatter | solution.py:83
  160.7 13.2 %all_to_all.25 = bf16[8,16,512]{2,1,0:T(8,128)(2,1)S(1)} all-to-all(bf16[8,16,512]{2,1,0:T(8,128)(2,1)} %bitcast.26), channel_id=1, replica_groups=mesh['seq'=2,'hist'=8,'chan'=2] {'hist'}, dimensions={0} | all-to-all | bytes 262144 | tf_op jit(solution)/shard_map/all_to_all | solution.py:84
  173.9 0.7 copy.9
  (3 shorter events, 0.0 us)
Async XLA Ops:
  6.5 145.8 %copy-start = (bf16[2048,512]{1,0:T(8,128)(2,1)S(1)}, bf16[2048,512]{1,0:T(8,128)(2,1)}, u32[]{:S(2)}) copy-start(bf16[2048,512]{1,0:T(8,128)(2,1)} %param.7) | copy-start | bytes 6291460
  6.5 6.1 %copy-start.1 = (bf16[256,2048]{1,0:T(8,128)(2,1)S(1)}, bf16[256,2048]{1,0:T(8,128)(2,1)}, u32[]{:S(2)}) copy-start(bf16[256,2048]{1,0:T(8,128)(2,1)} %param.4) | copy-start | bytes 3145732
  6.5 117.3 %reduce-scatter.3.cloned.1.call-start = ((), (), s32[]{:S(2)}) async-start(), calls=%async_computation.4 | async-start | bytes 2359296 | tf_op jit(solution)/shard_map/reduce_scatter | solution.py:61
  6.5 28.5 %collective-permute-start = (bf16[256,2048]{1,0:T(8,128)(2,1)}, bf16[256,2048]{1,0:T(8,128)(2,1)S(1)}, u32[]{:S(2)}, u32[]{:S(2)}) collective-permute-start(bf16[256,2048]{1,0:T(8,128)(2,1)} %param.5), channel_id=1, source_target_pairs={{2,0},{4,2},{6,4},{8,6},{10,8},{12,10},{14,12},{3,1},{5,3},{7,5},{... | collective-permute-start | bytes 3145736 | tf_op jit(solution)/shard_map/ppermute | solution.py:11
  12.6 1.3 copy-start.2
  46.1 77.7 %copy-start.3 = (bf16[32,2048]{1,0:T(8,128)(2,1)S(1)}, bf16[32,2048]{1,0:T(8,128)(2,1)}, u32[]{:S(2)}) copy-start(bf16[32,2048]{1,0:T(8,128)(2,1)} %param.6) | copy-start | bytes 393220
  53.6 107.0 %reduce-scatter.5.cloned.1.call-start = ((), (), s32[]{:S(2)}) async-start(), calls=%async_computation.5 | async-start | bytes 393216 | tf_op jit(solution)/shard_map/reduce_scatter | solution.py:83
Sparse Core Ops, SparseCore 0:
  53.8 70.0 reduce-scatter.2
  153.9 6.7 reduce-scatter.4
